TPU v7x, 32 devices: a whole 2x2x4 slice. The times are simulated.
32 devices in a mesh: layer: 2 (over core), latent: 8 (over z, x), token: 2 (over y).
Axes of the slice: x: 2, y: 2, z: 4, core: 2. Of those that a mesh axis runs over, the one named last changes fastest.
Arguments:
- taps: bfloat16 [2, 448, 3584], P('layer', 'token'), may hold values from -6 to 6
- token_ids: int32 [448], P('token'), may hold values from 2 to 255999, as said below
- enc_weight: bfloat16 [2, 3584, 2048], P('layer', 'token', 'latent'), may hold values from -0.0625 to 0.0625
- enc_bias: float32 [2048], P('latent'), may hold values from -3 to 3
- dec_weight: bfloat16 [2, 3584, 2048], P('layer', 'token', 'latent'), as said below
- dec_bias: float32 [2, 3584], P('layer'), may hold values from -3 to 3
Outputs:
- enc_grad: bfloat16 [2, 3584, 2048], P('layer', 'token', 'latent')
- dec_grad: bfloat16 [2, 3584, 2048], P('layer', 'token', 'latent')
Inputs may be any that keep to these rules, and one draw needn't show every extreme that they name: `token_ids`: id 2 marks the beginning of a document and stands at position 0; all other ids are 3 or more. `dec_weight`: entries of order 2048^-0.5.
All inputs are finite; a program needn't handle non-finite values.
Results may differ from a plain program's by a relative error of at most 0.014.
Values may be sent and summed in bfloat16 or wider, within the bound.
No kernel may reach another device: no remote copies, remote signals or barrier semaphores. Data moves between devices by JAX's collectives and lax.ppermute only.
A program may use at most 64 MiB of HBM per device.

v0:
```python
import math

import jax
import jax.numpy as jnp
from jax import lax
from jax.sharding import PartitionSpec as P


KNEE_WIDTH = 0.5
SPARSITY = 0.5
BEGIN_TOKEN = 2
BF = jnp.bfloat16
F32 = jnp.float32


def smooth_relu(preact):
    positive = jnp.maximum(preact, 0.0)
    return jnp.where(
        positive < KNEE_WIDTH, positive * positive / (2.0 * KNEE_WIDTH), positive - 0.5 * KNEE_WIDTH
    )


def relu_slope(preact):
    return jnp.clip(preact / KNEE_WIDTH, 0.0, 1.0)


def general(taps, token_ids, enc_weight, enc_bias, dec_weight, dec_bias):
    tap_rows = taps[0]
    tokens_dev = tap_rows.shape[0]
    latent_dev = enc_weight.shape[2]
    row_block = enc_weight.shape[1]
    loss_scale = 1.0 / math.sqrt(tokens_dev * lax.axis_size("token"))
    keep_mask = (token_ids != BEGIN_TOKEN).astype(jnp.float32)
    spread = lax.all_to_all(tap_rows, "token", split_axis=1, concat_axis=0, tiled=True)
    partial_pre = lax.psum_scatter(
        jnp.dot(spread, enc_weight[0], preferred_element_type=jnp.float32),
        "token",
        scatter_dimension=0,
        tiled=True,
    )
    preact = lax.psum(partial_pre, "layer") + enc_bias[None, :]
    features = smooth_relu(preact).astype(jnp.bfloat16)
    dec_full = lax.all_gather(dec_weight[0], "token", axis=0, tiled=True)
    rebuilt_part = lax.dot_general(
        features, dec_full, (((1,), (1,)), ((), ())), preferred_element_type=jnp.float32
    )
    rebuilt = lax.psum(rebuilt_part, "latent") + dec_bias[0][None, :]
    residue = (loss_scale * keep_mask[:, None] * (rebuilt - tap_rows.astype(jnp.float32))).astype(
        jnp.bfloat16
    )
    colnorm = jnp.sqrt(jnp.sum(jnp.square(dec_full.astype(jnp.float32)), axis=0) + 1e-06)
    back_part = jnp.dot(residue, dec_full, preferred_element_type=jnp.float32)
    feat_back, norm_total = lax.psum((back_part, colnorm), "layer")
    feat_grads = feat_back + loss_scale * SPARSITY * keep_mask[:, None] * norm_total[None, :]
    pre_grads = (feat_grads * relu_slope(preact)).astype(jnp.bfloat16)
    activity = jnp.sum(keep_mask[:, None] * features.astype(jnp.float32), axis=0)
    penalty_scale = loss_scale * SPARSITY * activity / colnorm
    product = lax.dot_general(
        residue, features, (((0,), (0,)), ((), ())), preferred_element_type=jnp.float32
    )
    dec_grad = lax.psum_scatter(
        (product + dec_full.astype(jnp.float32) * penalty_scale[None, :]).astype(jnp.bfloat16),
        "token",
        scatter_dimension=0,
        tiled=True,
    )
    code_rows = lax.all_gather(pre_grads, "token", axis=0, tiled=True)
    blocks = lax.axis_size("token")
    spread_blocks = spread.reshape(blocks, tokens_dev, row_block)
    code_blocks = code_rows.reshape(blocks, tokens_dev, latent_dev)
    block_terms = jnp.einsum(
        "btd,btk->bdk", spread_blocks, code_blocks, preferred_element_type=jnp.float32
    )
    enc_grad = jnp.sum(
        lax.optimization_barrier(block_terms.astype(jnp.bfloat16)).astype(jnp.float32), axis=0
    )
    return (enc_grad.astype(jnp.bfloat16)[None], dec_grad[None])


def flip(x, axis, bit):
    n = lax.axis_size(axis)
    return lax.ppermute(x, axis, [(i, i ^ bit) for i in range(n)])


def swap_core(x):
    return flip(x, "layer", 1)


def swap_tok(x):
    return flip(x, "token", 1)


def swap_both(x):
    return lax.ppermute(x, ("layer", "token"), [(i, i ^ 3) for i in range(4)])


def dot(a, b):
    return jnp.dot(a, b, preferred_element_type=F32)


def dot_t(a, b):
    return lax.dot_general(a, b, (((1,), (1,)), ((), ())), preferred_element_type=F32)


def dot_rows(a, b):
    return lax.dot_general(a, b, (((0,), (0,)), ((), ())), preferred_element_type=F32)


def pick(flag, first, second):
    return jnp.where(flag == 0, first, second)


def folded(taps, token_ids, enc_weight, enc_bias, dec_weight, dec_bias):
    return folded_body(taps, token_ids, enc_weight, enc_bias, dec_weight, dec_bias)


def folded_body(taps, token_ids, enc_weight, enc_bias, dec_weight, dec_bias):
    taps, enc_w, dec_w = taps[0], enc_weight[0], dec_weight[0]
    block, _ = taps.shape
    half_d = enc_w.shape[0]
    quarter_d = half_d // 2
    half_t = block // 2
    sub_t = half_t // 2
    scale = 1.0 / math.sqrt(block * lax.axis_size("token"))
    tok, core, lat = (lax.axis_index(a) for a in ("token", "layer", "latent"))
    xb, nb, fb = lat & 1, (lat >> 1) & 1, (lat >> 2) & 1
    swap_x = lambda v: flip(v, "latent", 1)
    swap_n = lambda v: flip(v, "latent", 2)
    swap_f = lambda v: flip(v, "latent", 4)
    sub_at = (nb, 1 - nb)

    def sub_rows(which_core, sub, which_half):
        at = which_core * half_t + sub_at[sub] * sub_t
        return lax.dynamic_slice(taps, (at, which_half * half_d), (sub_t, half_d))

    def core_rows(which_core):
        return lax.dynamic_slice(taps, (which_core * half_t, tok * half_d), (half_t, half_d))

    def after(v):
        nonlocal taps
        taps, v = lax.optimization_barrier((taps, v))
        return v

    d1 = swap_both(after(sub_rows(1 - core, 1, 1 - tok)))
    s1 = swap_tok(after(sub_rows(core, 1, 1 - tok)))
    enc_o = swap_core(enc_w)
    own_rest = after(core_rows(1 - core))
    t_core = swap_core(own_rest)
    own_mine = after(core_rows(core))
    d0 = swap_both(after(sub_rows(1 - core, 0, 1 - tok)))
    s0 = swap_tok(after(sub_rows(core, 0, 1 - tok)))
    dec_o = swap_core(dec_w)
    bias_o = swap_core(dec_bias)

    def by_sub(v):
        halves = v[:sub_t], v[sub_t:]
        return pick(nb, *halves), pick(nb, halves[1], halves[0])

    pre_own = dot(own_mine, enc_w) + dot(t_core, enc_o)
    far_oth = by_sub(swap_tok(pre_own.astype(BF)).astype(F32))
    pre_own = by_sub(pre_own)

    def activate(s, same, diag, earlier=None):
        pre_oth = dot(same, enc_w) + dot(diag, enc_o)
        far = swap_tok(pre_oth.astype(BF))
        if earlier is not None:
            far, _ = lax.optimization_barrier((far, earlier))
        own = pre_own[s] + far.astype(F32)
        oth = pre_oth + far_oth[s]
        pre = [pick(xb, own, oth) + enc_bias[None, :], pick(xb, oth, own) + enc_bias[None, :]]
        return pre, [smooth_relu(p).astype(BF) for p in pre]

    (p1, p3), (f1, f3) = activate(1, s1, d1)
    a3 = swap_x(dot_t(f3, dec_w).astype(BF))
    b3 = swap_n(dot_t(f3, dec_o).astype(BF))
    b1 = swap_n(dot_t(f1, dec_o).astype(BF))
    a1 = swap_n((dot_t(f1, dec_w) + a3.astype(F32)).astype(BF))
    (p0, p2), (f0, f2) = activate(0, s0, d0, f3)
    a2 = swap_x(dot_t(f2, dec_w).astype(BF))
    b2 = swap_x((dot_t(f2, dec_o) + b3.astype(F32)).astype(BF))
    preact = jnp.concatenate([p0, p1, p2, p3], 0)
    feats = jnp.concatenate(lax.optimization_barrier((f0, f1, f2, f3)), 0)

    keep_all = (token_ids != BEGIN_TOKEN).astype(F32)
    sq = jnp.sum(jnp.square(dec_w.astype(F32)), axis=0)
    small = jnp.concatenate([keep_all, sq])
    small_far = swap_tok(small)
    keep_far = small_far[:block]
    colnorm = jnp.sqrt(sq + small_far[block:] + 1e-06)
    norm_total = colnorm + swap_core(colnorm)
    keep_sub = lambda v, s: lax.dynamic_slice(v, (core * half_t + sub_at[s] * sub_t,), (sub_t,))
    keeps = [[keep_sub(v, s) for s in (0, 1)] for v in (keep_all, keep_far)]
    keep = jnp.concatenate(
        [pick(xb, keeps[0][s], keeps[1][s]) for s in (0, 1)]
        + [pick(xb, keeps[1][s], keeps[0][s]) for s in (0, 1)]
    )
    tap_at = lambda v: lax.dynamic_slice(v, (nb * sub_t, fb * quarter_d), (sub_t, quarter_d))

    def shard(v, at):
        return lax.dynamic_slice_in_dim(v, at * quarter_d, quarter_d, 1)

    keep0 = keep[:sub_t]
    tap_a = pick(xb, tap_at(own_mine), shard(s0, fb))
    tap_b = pick(xb, tap_at(t_core), shard(d0, fb))

    def finish(sum0, tap, bias, earlier=None):
        far = swap_f(shard(sum0, 1 - fb).astype(BF))
        if earlier is not None:
            far, _ = lax.optimization_barrier((far, earlier))
        rebuilt = shard(sum0, fb) + far.astype(F32)
        bias = lax.dynamic_slice(bias[0], (tok * half_d + fb * quarter_d,), (quarter_d,))
        res = scale * keep0[:, None] * (rebuilt + bias[None, :] - tap.astype(F32))
        res = res.astype(BF)
        far = swap_f(res)
        return res, jnp.concatenate([pick(fb, res, far), pick(fb, far, res)], 1)

    res, ra0 = finish(dot_t(f0, dec_w) + a1.astype(F32) + a2.astype(F32), tap_a, dec_bias)
    _, rb0 = finish(dot_t(f0, dec_o) + b1.astype(F32) + b2.astype(F32), tap_b, bias_o, res)
    ra2, ra1 = swap_x(ra0), swap_n(ra0)
    rb2, rb1 = swap_x(rb0), swap_n(rb0)
    ra3 = swap_x(ra1)
    rb3 = swap_n(rb2)
    res_a = jnp.concatenate([ra0, ra1, ra2, ra3], 0)
    res_b = jnp.concatenate([rb0, rb1, rb2, rb3], 0)
    res_o = swap_core(res_b)

    back = dot(res_a, dec_w) + dot(res_b, dec_o)
    back_far = swap_tok(back.astype(BF))
    back_far = jnp.concatenate([back_far[half_t:], back_far[:half_t]], 0).astype(F32)
    fg = back + back_far + scale * SPARSITY * keep[:, None] * norm_total[None, :]
    pre_g = (fg * relu_slope(preact)).astype(BF)

    feats_o = swap_core(feats)
    active = swap_core(jnp.sum(keep[:, None] * feats.astype(F32), axis=0))
    activity = jnp.sum(keep[:, None] * feats.astype(F32), axis=0) + active
    penalty = scale * SPARSITY * activity / colnorm
    prod = dot_rows(jnp.concatenate([res_a, res_o], 0), jnp.concatenate([feats, feats_o], 0))
    dec_grad = (prod + dec_w.astype(F32) * penalty[None, :]).astype(BF)

    pg = [pre_g[g * sub_t : (g + 1) * sub_t] for g in range(4)]
    pg_own = [pick(xb, pg[0], pg[2]), pick(xb, pg[1], pg[3])]
    pg_oth = [pick(xb, pg[2], pg[0]), pick(xb, pg[3], pg[1])]
    pg_own = [pick(nb, *pg_own), pick(nb, pg_own[1], pg_own[0])]
    pg = jnp.concatenate(pg_own + pg_oth, 0)
    pg_o = swap_core(pg)
    rest0, rest1 = swap_core(d0), swap_core(d1)
    tap_rows = jnp.concatenate([own_mine, s0, s1, own_rest, rest0, rest1], 0)
    enc_grad = dot_rows(tap_rows, jnp.concatenate([pg, pg_o], 0)).astype(BF)
    return (enc_grad[None], dec_grad[None])


def solution(mesh):
    placed = (
        P("layer", "token", None),
        P("token"),
        P("layer", "token", "latent"),
        P("latent"),
        P("layer", "token", "latent"),
        P("layer", None),
    )
    shape = dict(mesh.shape)
    foldable = shape["layer"] == 2 and shape["token"] == 2 and shape["latent"] == 8
    return jax.shard_map(
        folded if foldable else general,
        mesh=mesh,
        in_specs=placed,
        out_specs=(P("layer", "token", "latent"), P("layer", "token", "latent")),
        check_vma=False,
    )
```

profile of v0, /device:TPU:0, one launch (start us, length us, event | category | flops | bytes accessed | tf_op | source)
XLA Modules:
  0.0 109.6 jit_solution(8062408162774612678)
XLA Ops:
  8.7 3.0 %collective-permute-start = (bf16[56,1792]{1,0:T(8,128)(2,1)}, bf16[56,1792]{1,0:T(8,128)(2,1)S(1)}, u32[]{:S(2)}, u32[]{:S(2)}) collective-permute-start(bf16[56,1792]{1,0:T(8,128)(2,1)} %dynamic_slice.68), channel_id=1, source_target_pairs={{0,1},{1,0},{2,3},{3,2},{4,5},{5,4},{6,7},{7,6},{8,9},{9,8},{10,11... | collective-permute-start | bytes 602120 | tf_op jit(solution)/shard_map/ppermute | solution.py:82
  16.6 9.0 %collective-permute-done.6 = f32[480]{0:T(512)} collective-permute-done((f32[480]{0:T(512)}, f32[480]{0:T(512)}, u32[]{:S(2)}, u32[]{:S(2)}) %collective-permute-start.6) | collective-permute-done | bytes 1952 | tf_op jit(solution)/shard_map/ppermute | solution.py:82
  27.4 1.7 %collective-permute-start.8 = (bf16[1792,256]{1,0:T(8,128)(2,1)S(1)}, bf16[1792,256]{1,0:T(8,128)(2,1)S(1)}, u32[]{:S(2)}, u32[]{:S(2)}) collective-permute-start(bf16[1792,256]{1,0:T(8,128)(2,1)S(1)} %bitcast.65), channel_id=1, source_target_pairs={{0,16},{16,0},{1,17},{17,1},{2,18},{18,2},{3,19},{19,3},{4,20},{20... | collective-permute-start | bytes 2752520 | tf_op jit(solution)/shard_map/ppermute | solution.py:82
  43.5 2.1 %collective-permute-start.22 = (bf16[56,1792]{1,0:T(8,128)(2,1)S(1)}, bf16[56,1792]{1,0:T(8,128)(2,1)S(1)}, u32[]{:S(2)}, u32[]{:S(2)}) collective-permute-start(bf16[56,1792]{1,0:T(8,128)(2,1)S(1)} %convolution_convert_fusion.1), channel_id=1, source_target_pairs={{0,4},{2,6},{4,0},{6,2},{8,12},{10,14},{12,8},{14,10},{1,5},{3,7},... | collective-permute-start | bytes 602120 | tf_op jit(solution)/shard_map/ppermute | solution.py:82
  46.1 1.9 %collective-permute-start.12 = (bf16[56,1792]{1,0:T(8,128)(2,1)S(1)}, bf16[56,1792]{1,0:T(8,128)(2,1)S(1)}, u32[]{:S(2)}, u32[]{:S(2)}) collective-permute-start(bf16[56,1792]{1,0:T(8,128)(2,1)S(1)} %convolution_convert_fusion.4), channel_id=1, source_target_pairs={{0,2},{2,0},{4,6},{6,4},{8,10},{10,8},{12,14},{14,12},{1,3},{3,1},... | collective-permute-start | bytes 602120 | tf_op jit(solution)/shard_map/ppermute | solution.py:82
  48.7 3.2 %collective-permute-done.12 = bf16[56,1792]{1,0:T(8,128)(2,1)S(1)} collective-permute-done((bf16[56,1792]{1,0:T(8,128)(2,1)S(1)}, bf16[56,1792]{1,0:T(8,128)(2,1)S(1)}, u32[]{:S(2)}, u32[]{:S(2)}) %collective-permute-start.12) | collective-permute-done | bytes 200736 | tf_op jit(solution)/shard_map/ppermute | solution.py:82
  51.9 2.0 %collective-permute-start.14 = (bf16[56,1792]{1,0:T(8,128)(2,1)S(1)}, bf16[56,1792]{1,0:T(8,128)(2,1)S(1)}, u32[]{:S(2)}, u32[]{:S(2)}) collective-permute-start(bf16[56,1792]{1,0:T(8,128)(2,1)S(1)} %convolution_convert_fusion.3), channel_id=1, source_target_pairs={{0,2},{2,0},{4,6},{6,4},{8,10},{10,8},{12,14},{14,12},{1,3},{3,1},... | collective-permute-start | bytes 602120 | tf_op jit(solution)/shard_map/ppermute | solution.py:82
  57.6 2.5 %collective-permute-done.13 = bf16[56,1792]{1,0:T(8,128)(2,1)S(1)} collective-permute-done((bf16[56,1792]{1,0:T(8,128)(2,1)S(1)}, bf16[56,1792]{1,0:T(8,128)(2,1)S(1)}, u32[]{:S(2)}, u32[]{:S(2)}) %collective-permute-start.13) | collective-permute-done | bytes 200736 | tf_op jit(solution)/shard_map/ppermute | solution.py:82
  60.7 3.1 %collective-permute-start.15 = (bf16[56,896]{1,0:T(8,128)(2,1)S(1)}, bf16[56,896]{1,0:T(8,128)(2,1)S(1)}, u32[]{:S(2)}, u32[]{:S(2)}) collective-permute-start(bf16[56,896]{1,0:T(8,128)(2,1)S(1)} %dynamic-slice_convert_fusion.1), channel_id=1, source_target_pairs={{0,8},{2,10},{4,12},{6,14},{8,0},{10,2},{12,4},{14,6},{1,9},{3,11}... | collective-permute-start | bytes 301064 | tf_op jit(solution)/shard_map/ppermute | solution.py:82
  63.8 2.0 %collective-permute-done.23 = bf16[56,1792]{1,0:T(8,128)(2,1)S(1)} collective-permute-done((bf16[56,1792]{1,0:T(8,128)(2,1)S(1)}, bf16[56,1792]{1,0:T(8,128)(2,1)S(1)}, u32[]{:S(2)}, u32[]{:S(2)}) %collective-permute-start.23) | collective-permute-done | bytes 200736 | tf_op jit(solution)/shard_map/ppermute | solution.py:82
  66.3 2.6 %collective-permute-start.24 = (bf16[56,896]{1,0:T(8,128)(2,1)S(1)}, bf16[56,896]{1,0:T(8,128)(2,1)S(1)}, u32[]{:S(2)}, u32[]{:S(2)}) collective-permute-start(bf16[56,896]{1,0:T(8,128)(2,1)S(1)} %dynamic-slice_convert_fusion), channel_id=1, source_target_pairs={{0,8},{2,10},{4,12},{6,14},{8,0},{10,2},{12,4},{14,6},{1,9},{3,11}... | collective-permute-start | bytes 301064 | tf_op jit(solution)/shard_map/ppermute | solution.py:82
  69.7 2.2 %collective-permute-done.24 = bf16[56,896]{1,0:T(8,128)(2,1)S(1)} collective-permute-done((bf16[56,896]{1,0:T(8,128)(2,1)S(1)}, bf16[56,896]{1,0:T(8,128)(2,1)S(1)}, u32[]{:S(2)}, u32[]{:S(2)}) %collective-permute-start.24) | collective-permute-done | bytes 100384 | tf_op jit(solution)/shard_map/ppermute | solution.py:82
  72.0 2.9 %collective-permute-start.26 = (bf16[56,896]{1,0:T(8,128)(2,1)S(1)}, bf16[56,896]{1,0:T(8,128)(2,1)S(1)}, u32[]{:S(2)}, u32[]{:S(2)}) collective-permute-start(bf16[56,896]{1,0:T(8,128)(2,1)S(1)} %multiply_convert_fusion), channel_id=1, source_target_pairs={{0,8},{2,10},{4,12},{6,14},{8,0},{10,2},{12,4},{14,6},{1,9},{3,11}... | collective-permute-start | bytes 301064 | tf_op jit(solution)/shard_map/ppermute | solution.py:82
  75.8 1.8 %collective-permute-done.26 = bf16[56,896]{1,0:T(8,128)(2,1)S(1)} collective-permute-done((bf16[56,896]{1,0:T(8,128)(2,1)S(1)}, bf16[56,896]{1,0:T(8,128)(2,1)S(1)}, u32[]{:S(2)}, u32[]{:S(2)}) %collective-permute-start.26) | collective-permute-done | bytes 100384 | tf_op jit(solution)/shard_map/ppermute | solution.py:82
  77.7 4.1 %collective-permute-start.28 = (bf16[56,1792]{1,0:T(8,128)(2,1)S(1)}, bf16[56,1792]{1,0:T(8,128)(2,1)S(1)}, u32[]{:S(2)}, u32[]{:S(2)}) collective-permute-start(bf16[56,1792]{1,0:T(8,128)(2,1)S(1)} %pad_maximum_fusion.2), channel_id=1, source_target_pairs={{0,2},{2,0},{4,6},{6,4},{8,10},{10,8},{12,14},{14,12},{1,3},{3,1},... | collective-permute-start | bytes 602120 | tf_op jit(solution)/shard_map/ppermute | solution.py:82
  82.8 2.8 %collective-permute-start.17 = (bf16[56,1792]{1,0:T(8,128)(2,1)S(1)}, bf16[56,1792]{1,0:T(8,128)(2,1)S(1)}, u32[]{:S(2)}, u32[]{:S(2)}) collective-permute-start(bf16[56,1792]{1,0:T(8,128)(2,1)S(1)} %get-tuple-element.61), channel_id=1, source_target_pairs={{0,4},{2,6},{4,0},{6,2},{8,12},{10,14},{12,8},{14,10},{1,5},{3,7},... | collective-permute-start | bytes 602120 | tf_op jit(solution)/shard_map/ppermute | solution.py:82
  85.7 2.1 %collective-permute-start.18 = (bf16[56,1792]{1,0:T(8,128)(2,1)S(1)}, bf16[56,1792]{1,0:T(8,128)(2,1)S(1)}, u32[]{:S(2)}, u32[]{:S(2)}) collective-permute-start(bf16[56,1792]{1,0:T(8,128)(2,1)S(1)} %get-tuple-element.61), channel_id=1, source_target_pairs={{0,2},{2,0},{4,6},{6,4},{8,10},{10,8},{12,14},{14,12},{1,3},{3,1},... | collective-permute-start | bytes 602120 | tf_op jit(solution)/shard_map/ppermute | solution.py:82
  88.6 2.8 %collective-permute-done.17 = bf16[56,1792]{1,0:T(8,128)(2,1)S(1)} collective-permute-done((bf16[56,1792]{1,0:T(8,128)(2,1)S(1)}, bf16[56,1792]{1,0:T(8,128)(2,1)S(1)}, u32[]{:S(2)}, u32[]{:S(2)}) %collective-permute-start.17) | collective-permute-done | bytes 200736 | tf_op jit(solution)/shard_map/ppermute | solution.py:82
  91.4 2.1 %collective-permute-start.19 = (bf16[56,1792]{1,0:T(8,128)(2,1)S(1)}, bf16[56,1792]{1,0:T(8,128)(2,1)S(1)}, u32[]{:S(2)}, u32[]{:S(2)}) collective-permute-start(bf16[56,1792]{1,0:T(8,128)(2,1)S(1)} %collective-permute-done.17), channel_id=1, source_target_pairs={{0,2},{2,0},{4,6},{6,4},{8,10},{10,8},{12,14},{14,12},{1,3},{3,1},... | collective-permute-start | bytes 602120 | tf_op jit(solution)/shard_map/ppermute | solution.py:82
  93.5 2.2 %collective-permute-done.27 = bf16[56,1792]{1,0:T(8,128)(2,1)S(1)} collective-permute-done((bf16[56,1792]{1,0:T(8,128)(2,1)S(1)}, bf16[56,1792]{1,0:T(8,128)(2,1)S(1)}, u32[]{:S(2)}, u32[]{:S(2)}) %collective-permute-start.27) | collective-permute-done | bytes 200736 | tf_op jit(solution)/shard_map/ppermute | solution.py:82
  95.7 3.2 %collective-permute-done.29 = bf16[56,1792]{1,0:T(8,128)(2,1)S(1)} collective-permute-done((bf16[56,1792]{1,0:T(8,128)(2,1)S(1)}, bf16[56,1792]{1,0:T(8,128)(2,1)S(1)}, u32[]{:S(2)}, u32[]{:S(2)}) %collective-permute-start.29) | collective-permute-done | bytes 200736 | tf_op jit(solution)/shard_map/ppermute | solution.py:82
  100.3 4.2 %collective-permute-done.30 = bf16[224,256]{1,0:T(8,128)(2,1)S(1)} collective-permute-done((bf16[224,256]{1,0:T(8,128)(2,1)S(1)}, bf16[224,256]{1,0:T(8,128)(2,1)S(1)}, u32[]{:S(2)}, u32[]{:S(2)}) %collective-permute-start.30) | collective-permute-done | bytes 114720 | tf_op jit(solution)/shard_map/ppermute | solution.py:82
  106.2 1.7 %fusion.2 = bf16[1,1792,256]{2,1,0:T(8,128)(2,1)} fusion(bf16[448,1792]{1,0:T(8,128)(2,1)S(1)} %constant_dynamic-update-slice_fusion, bf16[448,256]{1,0:T(8,128)(2,1)S(1)} %constant_dynamic-update-slice_fusion.6), kind=kOutput, calls=%fused_computation.4 | convolution fusion | flops 411500544 | bytes 2752512 | tf_op jit(solution)/shard_map/dot_general | solution.py:106
  107.9 1.7 %fusion.1 = bf16[1,1792,256]{2,1,0:T(8,128)(2,1)} fusion(bf16[448,1792]{1,0:T(8,128)(2,1)S(1)} %constant_dynamic-update-slice_fusion.11, bf16[448,256]{1,0:T(8,128)(2,1)S(1)} %constant_dynamic-update-slice_fusion.20, f32[256]{0:T(256)S(1)} %get-tuple-element.36, bf16[1,1792,256]{2,1,0:T(8,128)(2,1)S(1)} %copy-done), kind=kOutput, calls=%fused_computation.3 | convolution fusion | flops 412876800 | bytes 3671040 | tf_op jit(solution)/shard_map/dot_general | solution.py:106
  (136 shorter events, 41.6 us)
Async XLA Ops:
  8.7 21.1 %collective-permute-start = (bf16[56,1792]{1,0:T(8,128)(2,1)}, bf16[56,1792]{1,0:T(8,128)(2,1)S(1)}, u32[]{:S(2)}, u32[]{:S(2)}) collective-permute-start(bf16[56,1792]{1,0:T(8,128)(2,1)} %dynamic_slice.68), channel_id=1, source_target_pairs={{0,1},{1,0},{2,3},{3,2},{4,5},{5,4},{6,7},{7,6},{8,9},{9,8},{10,11... | collective-permute-start | bytes 602120 | tf_op jit(solution)/shard_map/ppermute | solution.py:82
  11.7 18.9 %collective-permute-start.1 = (bf16[56,1792]{1,0:T(8,128)(2,1)}, bf16[56,1792]{1,0:T(8,128)(2,1)S(1)}, u32[]{:S(2)}, u32[]{:S(2)}) collective-permute-start(bf16[56,1792]{1,0:T(8,128)(2,1)} %dynamic_slice.64), channel_id=1, source_target_pairs={{0,1},{1,0},{2,3},{3,2},{4,5},{5,4},{6,7},{7,6},{8,9},{9,8},{10,11... | collective-permute-start | bytes 602120 | tf_op jit(solution)/shard_map/ppermute | solution.py:82
  11.7 19.4 %collective-permute-start.2 = (bf16[56,1792]{1,0:T(8,128)(2,1)}, bf16[56,1792]{1,0:T(8,128)(2,1)S(1)}, u32[]{:S(2)}, u32[]{:S(2)}) collective-permute-start(bf16[56,1792]{1,0:T(8,128)(2,1)} %dynamic_slice.67), channel_id=1, source_target_pairs={{0,17},{1,16},{16,1},{17,0},{2,19},{3,18},{18,3},{19,2},{4,21},{5,... | collective-permute-start | bytes 602120 | tf_op jit(solution)/shard_map/ppermute | solution.py:94
  13.6 12.1 %collective-permute-start.6 = (f32[480]{0:T(512)}, f32[480]{0:T(512)}, u32[]{:S(2)}, u32[]{:S(2)}) collective-permute-start(f32[480]{0:T(512)} %pad_maximum_fusion.4), channel_id=1, source_target_pairs={{0,1},{1,0},{2,3},{3,2},{4,5},{5,4},{6,7},{7,6},{8,9},{9,8},{10,11... | collective-permute-start | bytes 5768 | tf_op jit(solution)/shard_map/ppermute | solution.py:82
  14.7 12.7 %collective-permute-start.25 = (f32[1,3584]{1,0:T(1,128)}, f32[1,3584]{1,0:T(1,128)}, u32[]{:S(2)}, u32[]{:S(2)}) collective-permute-start(f32[1,3584]{1,0:T(1,128)} %param.11), channel_id=1, source_target_pairs={{0,16},{16,0},{1,17},{17,1},{2,18},{18,2},{3,19},{19,3},{4,20},{20... | collective-permute-start | bytes 43016 | tf_op jit(solution)/shard_map/ppermute | solution.py:82
  25.7 7.0 %collective-permute-start.4 = (bf16[56,1792]{1,0:T(8,128)(2,1)S(1)}, bf16[56,1792]{1,0:T(8,128)(2,1)S(1)}, u32[]{:S(2)}, u32[]{:S(2)}) collective-permute-start(bf16[56,1792]{1,0:T(8,128)(2,1)S(1)} %dynamic-slice_bitcast_fusion), channel_id=1, source_target_pairs={{0,17},{1,16},{16,1},{17,0},{2,19},{3,18},{18,3},{19,2},{4,21},{5,... | collective-permute-start | bytes 602120 | tf_op jit(solution)/shard_map/ppermute | solution.py:94
  27.4 7.5 %collective-permute-start.8 = (bf16[1792,256]{1,0:T(8,128)(2,1)S(1)}, bf16[1792,256]{1,0:T(8,128)(2,1)S(1)}, u32[]{:S(2)}, u32[]{:S(2)}) collective-permute-start(bf16[1792,256]{1,0:T(8,128)(2,1)S(1)} %bitcast.65), channel_id=1, source_target_pairs={{0,16},{16,0},{1,17},{17,1},{2,18},{18,2},{3,19},{19,3},{4,20},{20... | collective-permute-start | bytes 2752520 | tf_op jit(solution)/shard_map/ppermute | solution.py:82
  29.8 6.8 %collective-permute-start.7 = (bf16[112,1792]{1,0:T(8,128)(2,1)S(1)}, bf16[112,1792]{1,0:T(8,128)(2,1)S(1)}, u32[]{:S(2)}, u32[]{:S(2)}) collective-permute-start(bf16[112,1792]{1,0:T(8,128)(2,1)S(1)} %dynamic_slice.65), channel_id=1, source_target_pairs={{0,16},{16,0},{1,17},{17,1},{2,18},{18,2},{3,19},{19,3},{4,20},{20... | collective-permute-start | bytes 1204232 | tf_op jit(solution)/shard_map/ppermute | solution.py:82
  30.6 12.5 %collective-permute-start.20 = (bf16[1792,256]{1,0:T(8,128)(2,1)S(1)}, bf16[1792,256]{1,0:T(8,128)(2,1)S(1)}, u32[]{:S(2)}, u32[]{:S(2)}) collective-permute-start(bf16[1792,256]{1,0:T(8,128)(2,1)S(1)} %bitcast.64), channel_id=1, source_target_pairs={{0,16},{16,0},{1,17},{17,1},{2,18},{18,2},{3,19},{19,3},{4,20},{20... | collective-permute-start | bytes 2752520 | tf_op jit(solution)/shard_map/ppermute | solution.py:82
  32.7 52.9 %collective-permute-start.5 = (bf16[56,1792]{1,0:T(8,128)(2,1)S(1)}, bf16[56,1792]{1,0:T(8,128)(2,1)S(1)}, u32[]{:S(2)}, u32[]{:S(2)}) collective-permute-start(bf16[56,1792]{1,0:T(8,128)(2,1)S(1)} %collective-permute-done.4), channel_id=1, source_target_pairs={{0,16},{16,0},{1,17},{17,1},{2,18},{18,2},{3,19},{19,3},{4,20},{20... | collective-permute-start | bytes 602120 | tf_op jit(solution)/shard_map/ppermute | solution.py:82
  43.5 10.8 %collective-permute-start.22 = (bf16[56,1792]{1,0:T(8,128)(2,1)S(1)}, bf16[56,1792]{1,0:T(8,128)(2,1)S(1)}, u32[]{:S(2)}, u32[]{:S(2)}) collective-permute-start(bf16[56,1792]{1,0:T(8,128)(2,1)S(1)} %convolution_convert_fusion.1), channel_id=1, source_target_pairs={{0,4},{2,6},{4,0},{6,2},{8,12},{10,14},{12,8},{14,10},{1,5},{3,7},... | collective-permute-start | bytes 602120 | tf_op jit(solution)/shard_map/ppermute | solution.py:82
  46.0 14.6 %collective-permute-start.21 = (bf16[56,1792]{1,0:T(8,128)(2,1)S(1)}, bf16[56,1792]{1,0:T(8,128)(2,1)S(1)}, u32[]{:S(2)}, u32[]{:S(2)}) collective-permute-start(bf16[56,1792]{1,0:T(8,128)(2,1)S(1)} %convolution_convert_fusion.2), channel_id=1, source_target_pairs={{0,4},{2,6},{4,0},{6,2},{8,12},{10,14},{12,8},{14,10},{1,5},{3,7},... | collective-permute-start | bytes 602120 | tf_op jit(solution)/shard_map/ppermute | solution.py:82
  48.1 37.5 %collective-permute-start.34 = (bf16[224,256]{1,0:T(8,128)(2,1)S(1)}, bf16[224,256]{1,0:T(8,128)(2,1)S(1)}, u32[]{:S(2)}, u32[]{:S(2)}) collective-permute-start(bf16[224,256]{1,0:T(8,128)(2,1)S(1)} %get-tuple-element.69), channel_id=1, source_target_pairs={{0,16},{16,0},{1,17},{17,1},{2,18},{18,2},{3,19},{19,3},{4,20},{20... | collective-permute-start | bytes 344072 | tf_op jit(solution)/shard_map/ppermute | solution.py:82
  57.6 17.3 %collective-permute-start.35 = (f32[256]{0:T(256)S(1)}, f32[256]{0:T(256)S(1)}, u32[]{:S(2)}, u32[]{:S(2)}) collective-permute-start(f32[256]{0:T(256)S(1)} %multiply_reduce_fusion), channel_id=1, source_target_pairs={{0,16},{16,0},{1,17},{17,1},{2,18},{18,2},{3,19},{19,3},{4,20},{20... | collective-permute-start | bytes 3080 | tf_op jit(solution)/shard_map/ppermute | solution.py:82
  60.7 8.9 %collective-permute-start.15 = (bf16[56,896]{1,0:T(8,128)(2,1)S(1)}, bf16[56,896]{1,0:T(8,128)(2,1)S(1)}, u32[]{:S(2)}, u32[]{:S(2)}) collective-permute-start(bf16[56,896]{1,0:T(8,128)(2,1)S(1)} %dynamic-slice_convert_fusion.1), channel_id=1, source_target_pairs={{0,8},{2,10},{4,12},{6,14},{8,0},{10,2},{12,4},{14,6},{1,9},{3,11}... | collective-permute-start | bytes 301064 | tf_op jit(solution)/shard_map/ppermute | solution.py:82
  75.6 9.9 %collective-permute-start.31 = (f32[256]{0:T(256)S(1)}, f32[256]{0:T(256)S(1)}, u32[]{:S(2)}, u32[]{:S(2)}) collective-permute-start(f32[256]{0:T(256)S(1)} %get-tuple-element.37), channel_id=1, source_target_pairs={{0,16},{16,0},{1,17},{17,1},{2,18},{18,2},{3,19},{19,3},{4,20},{20... | collective-permute-start | bytes 3080 | tf_op jit(solution)/shard_map/ppermute | solution.py:82
  75.6 7.1 %collective-permute-start.16 = (bf16[56,896]{1,0:T(8,128)(2,1)S(1)}, bf16[56,896]{1,0:T(8,128)(2,1)S(1)}, u32[]{:S(2)}, u32[]{:S(2)}) collective-permute-start(bf16[56,896]{1,0:T(8,128)(2,1)S(1)} %multiply_convert_fusion.1), channel_id=1, source_target_pairs={{0,8},{2,10},{4,12},{6,14},{8,0},{10,2},{12,4},{14,6},{1,9},{3,11}... | collective-permute-start | bytes 301064 | tf_op jit(solution)/shard_map/ppermute | solution.py:82
  77.7 10.1 %collective-permute-start.28 = (bf16[56,1792]{1,0:T(8,128)(2,1)S(1)}, bf16[56,1792]{1,0:T(8,128)(2,1)S(1)}, u32[]{:S(2)}, u32[]{:S(2)}) collective-permute-start(bf16[56,1792]{1,0:T(8,128)(2,1)S(1)} %pad_maximum_fusion.2), channel_id=1, source_target_pairs={{0,2},{2,0},{4,6},{6,4},{8,10},{10,8},{12,14},{14,12},{1,3},{3,1},... | collective-permute-start | bytes 602120 | tf_op jit(solution)/shard_map/ppermute | solution.py:82
  82.8 8.6 %collective-permute-start.17 = (bf16[56,1792]{1,0:T(8,128)(2,1)S(1)}, bf16[56,1792]{1,0:T(8,128)(2,1)S(1)}, u32[]{:S(2)}, u32[]{:S(2)}) collective-permute-start(bf16[56,1792]{1,0:T(8,128)(2,1)S(1)} %get-tuple-element.61), channel_id=1, source_target_pairs={{0,4},{2,6},{4,0},{6,2},{8,12},{10,14},{12,8},{14,10},{1,5},{3,7},... | collective-permute-start | bytes 602120 | tf_op jit(solution)/shard_map/ppermute | solution.py:82
  85.6 10.1 %collective-permute-start.27 = (bf16[56,1792]{1,0:T(8,128)(2,1)S(1)}, bf16[56,1792]{1,0:T(8,128)(2,1)S(1)}, u32[]{:S(2)}, u32[]{:S(2)}) collective-permute-start(bf16[56,1792]{1,0:T(8,128)(2,1)S(1)} %pad_maximum_fusion.2), channel_id=1, source_target_pairs={{0,4},{2,6},{4,0},{6,2},{8,12},{10,14},{12,8},{14,10},{1,5},{3,7},... | collective-permute-start | bytes 602120 | tf_op jit(solution)/shard_map/ppermute | solution.py:82
  85.7 13.6 %collective-permute-start.18 = (bf16[56,1792]{1,0:T(8,128)(2,1)S(1)}, bf16[56,1792]{1,0:T(8,128)(2,1)S(1)}, u32[]{:S(2)}, u32[]{:S(2)}) collective-permute-start(bf16[56,1792]{1,0:T(8,128)(2,1)S(1)} %get-tuple-element.61), channel_id=1, source_target_pairs={{0,2},{2,0},{4,6},{6,4},{8,10},{10,8},{12,14},{14,12},{1,3},{3,1},... | collective-permute-start | bytes 602120 | tf_op jit(solution)/shard_map/ppermute | solution.py:82
  87.8 11.1 %collective-permute-start.29 = (bf16[56,1792]{1,0:T(8,128)(2,1)S(1)}, bf16[56,1792]{1,0:T(8,128)(2,1)S(1)}, u32[]{:S(2)}, u32[]{:S(2)}) collective-permute-start(bf16[56,1792]{1,0:T(8,128)(2,1)S(1)} %collective-permute-done.28), channel_id=1, source_target_pairs={{0,4},{2,6},{4,0},{6,2},{8,12},{10,14},{12,8},{14,10},{1,5},{3,7},... | collective-permute-start | bytes 602120 | tf_op jit(solution)/shard_map/ppermute | solution.py:82
  91.4 7.9 %collective-permute-start.19 = (bf16[56,1792]{1,0:T(8,128)(2,1)S(1)}, bf16[56,1792]{1,0:T(8,128)(2,1)S(1)}, u32[]{:S(2)}, u32[]{:S(2)}) collective-permute-start(bf16[56,1792]{1,0:T(8,128)(2,1)S(1)} %collective-permute-done.17), channel_id=1, source_target_pairs={{0,2},{2,0},{4,6},{6,4},{8,10},{10,8},{12,14},{14,12},{1,3},{3,1},... | collective-permute-start | bytes 602120 | tf_op jit(solution)/shard_map/ppermute | solution.py:82
  100.2 7.6 %collective-permute-start.33 = (bf16[224,1792]{1,0:T(8,128)(2,1)S(1)}, bf16[224,1792]{1,0:T(8,128)(2,1)S(1)}, u32[]{:S(2)}, u32[]{:S(2)}) collective-permute-start(bf16[224,1792]{1,0:T(8,128)(2,1)S(1)} %pad_maximum_fusion), channel_id=1, source_target_pairs={{0,16},{16,0},{1,17},{17,1},{2,18},{18,2},{3,19},{19,3},{4,20},{20... | collective-permute-start | bytes 2408456 | tf_op jit(solution)/shard_map/ppermute | solution.py:82
  (20 other events, 131.9 us)
where the time goes:
time: 110 us
  waiting for transfers between devices  41.6 us (38%)
  starting transfers between devices  40.3 us (37%)
  local copies, waits for them, and re-layouts  14 us (13%)
  matrix products  9.25 us (8%)
  other arithmetic  3.36 us (3%)
  between operations  1.14 us (1%)
    ppermute x34, waiting for transfers between devices, flip(): return lax.ppermute(x, axis, [(i, i ^ bit) for i in range(n)])  40.1 us
    ppermute x34, starting transfers between devices, flip(): return lax.ppermute(x, axis, [(i, i ^ bit) for i in range(n)])  39.2 us
    dynamic_slice x4, local copies, waits for them, and re-layouts, sub_rows(): return lax.dynamic_slice(taps, (at, which_half * half_d), (sub_t, half_d))  5.91 us
    unnamed x28, local copies, waits for them, and re-layouts  3.78 us
    dot_general x8, matrix products, dot_t(): lax.dot_general(a, b, (((1,), (1,)), ((), ())), preferred_element_type=F32)  3.42 us
    dot_general x2, matrix products, dot_rows(): lax.dot_general(a, b, (((0,), (0,)), ((), ())), preferred_element_type=F32)  3.31 us
    dot_general x8, matrix products, dot(): return jnp.dot(a, b, preferred_element_type=F32)  2.52 us
  transfers between devices with their start and end apart: 36, of which 17 were waited for; matrix products, arithmetic and copies ran while one was open for 15% of the time, Pallas kernels for 0%

commit v1 on v0

--- a/solution.py
+++ b/solution.py
@@ -136,19 +136,15 @@
     def core_rows(which_core):
         return lax.dynamic_slice(taps, (which_core * half_t, tok * half_d), (half_t, half_d))
 
-    def after(v):
-        nonlocal taps
-        taps, v = lax.optimization_barrier((taps, v))
-        return v
-
-    d1 = swap_both(after(sub_rows(1 - core, 1, 1 - tok)))
-    s1 = swap_tok(after(sub_rows(core, 1, 1 - tok)))
+    sent = (sub_rows(1 - core, 1, 1 - tok), sub_rows(core, 1, 1 - tok)) + (
+        sub_rows(1 - core, 0, 1 - tok), sub_rows(core, 0, 1 - tok)
+    )
+    taps, *sent = lax.optimization_barrier((taps, *sent))
+    d1, s1 = swap_both(sent[0]), swap_tok(sent[1])
     enc_o = swap_core(enc_w)
-    own_rest = after(core_rows(1 - core))
+    own_rest, own_mine = core_rows(1 - core), core_rows(core)
     t_core = swap_core(own_rest)
-    own_mine = after(core_rows(core))
-    d0 = swap_both(after(sub_rows(1 - core, 0, 1 - tok)))
-    s0 = swap_tok(after(sub_rows(core, 0, 1 - tok)))
+    d0, s0 = swap_both(sent[2]), swap_tok(sent[3])
     dec_o = swap_core(dec_w)
     bias_o = swap_core(dec_bias)
 
@@ -156,17 +152,22 @@
         halves = v[:sub_t], v[sub_t:]
         return pick(nb, *halves), pick(nb, halves[1], halves[0])
 
-    pre_own = dot(own_mine, enc_w) + dot(t_core, enc_o)
-    far_oth = by_sub(swap_tok(pre_own.astype(BF)).astype(F32))
+    enc_all = lax.optimization_barrier(jnp.concatenate([enc_w, enc_o], 0))
+
+    def encode(own_layer, other_layer):
+        return dot(own_layer, enc_all[:half_d]) + dot(other_layer, enc_all[half_d:])
+
+    pre_own = encode(own_mine, t_core)
+    far_oth = by_sub(swap_tok(pre_own.astype(BF)))
     pre_own = by_sub(pre_own)
 
     def activate(s, same, diag, earlier=None):
-        pre_oth = dot(same, enc_w) + dot(diag, enc_o)
+        pre_oth = encode(same, diag)
         far = swap_tok(pre_oth.astype(BF))
         if earlier is not None:
             far, _ = lax.optimization_barrier((far, earlier))
         own = pre_own[s] + far.astype(F32)
-        oth = pre_oth + far_oth[s]
+        oth = pre_oth + far_oth[s].astype(F32)
         pre = [pick(xb, own, oth) + enc_bias[None, :], pick(xb, oth, own) + enc_bias[None, :]]
         return pre, [smooth_relu(p).astype(BF) for p in pre]
 
@@ -178,16 +179,15 @@
     (p0, p2), (f0, f2) = activate(0, s0, d0, f3)
     a2 = swap_x(dot_t(f2, dec_w).astype(BF))
     b2 = swap_x((dot_t(f2, dec_o) + b3.astype(F32)).astype(BF))
-    preact = jnp.concatenate([p0, p1, p2, p3], 0)
-    feats = jnp.concatenate(lax.optimization_barrier((f0, f1, f2, f3)), 0)
-
+
+    token_ids, dec_late, dec_bias, bias_o, _ = lax.optimization_barrier(
+        (token_ids, dec_w, dec_bias, bias_o, f2)
+    )
     keep_all = (token_ids != BEGIN_TOKEN).astype(F32)
-    sq = jnp.sum(jnp.square(dec_w.astype(F32)), axis=0)
+    sq = jnp.sum(jnp.square(dec_late.astype(F32)), axis=0)
     small = jnp.concatenate([keep_all, sq])
     small_far = swap_tok(small)
     keep_far = small_far[:block]
-    colnorm = jnp.sqrt(sq + small_far[block:] + 1e-06)
-    norm_total = colnorm + swap_core(colnorm)
     keep_sub = lambda v, s: lax.dynamic_slice(v, (core * half_t + sub_at[s] * sub_t,), (sub_t,))
     keeps = [[keep_sub(v, s) for s in (0, 1)] for v in (keep_all, keep_far)]
     keep = jnp.concatenate(
@@ -216,6 +216,14 @@
 
     res, ra0 = finish(dot_t(f0, dec_w) + a1.astype(F32) + a2.astype(F32), tap_a, dec_bias)
     _, rb0 = finish(dot_t(f0, dec_o) + b1.astype(F32) + b2.astype(F32), tap_b, bias_o, res)
+
+    own_mine, own_rest, s0, s1, d0, d1, f0, f1, f2, f3, _ = lax.optimization_barrier(
+        (own_mine, own_rest, s0, s1, d0, d1, f0, f1, f2, f3, res)
+    )
+    preact = jnp.concatenate([p0, p1, p2, p3], 0)
+    feats = jnp.concatenate([f0, f1, f2, f3], 0)
+    colnorm = jnp.sqrt(sq + small_far[block:] + 1e-06)
+    norm_total = colnorm + swap_core(colnorm)
     ra2, ra1 = swap_x(ra0), swap_n(ra0)
     rb2, rb1 = swap_x(rb0), swap_n(rb0)
     ra3 = swap_x(ra1)

time: 110 us -> 102 us (0.927)
  local copies, waits for them, and re-layouts: 14 us -> 2.46 us
  waiting for transfers between devices: 41.6 us -> 51.2 us
  starting transfers between devices: 40.3 us -> 32.4 us
  matrix products: 9.25 us -> 11.1 us
    ppermute x2, waiting for transfers between devices: 1.49 us -> 13.6 us  [swap_both(): return lax.ppermute(x, ('layer', 'token'), [(i, i ^ 3) for i in range(4)])]
    ppermute x34, starting transfers between devices: 39.2 us -> 30.7 us  [flip(): return lax.ppermute(x, axis, [(i, i ^ bit) for i in range(n)])]
    dynamic_slice x4 -> x1, local copies, waits for them, and re-layouts: 5.91 us -> 2.03 us  [sub_rows(): return lax.dynamic_slice(taps, (at, which_half * half_d), (sub_t, half_d))]
    unnamed x28 -> x24, local copies, waits for them, and re-layouts: 3.78 us -> 0.2 us
    ppermute x34, waiting for transfers between devices: 40.1 us -> 37.6 us  [flip(): return lax.ppermute(x, axis, [(i, i ^ bit) for i in range(n)])]
    dynamic_slice x2 -> x1, local copies, waits for them, and re-layouts: 2.14 us -> 0.05 us  [core_rows(): lax.dynamic_slice(taps, (which_core * half_t, tok * half_d), (half_t, hal...]
    dot_general x8, matrix products: 2.52 us -> 4.37 us  [dot(): return jnp.dot(a, b, preferred_element_type=F32)]
    dynamic_slice x2, local copies, waits for them, and re-layouts: 1.38 us -> 0.04 us  [finish(): lax.dynamic_slice(bias[0], (tok * half_d + fb * quarter_d,), (quarter_d,))]
where the time goes in v1:
time: 102 us
  waiting for transfers between devices  51.2 us (50%)
  starting transfers between devices  32.4 us (32%)
  matrix products  11.1 us (11%)
  other arithmetic  3.6 us (4%)
  local copies, waits for them, and re-layouts  2.46 us (2%)
  between operations  1.13 us (1%)
    ppermute x34, waiting for transfers between devices, flip(): return lax.ppermute(x, axis, [(i, i ^ bit) for i in range(n)])  37.6 us
    ppermute x34, starting transfers between devices, flip(): return lax.ppermute(x, axis, [(i, i ^ bit) for i in range(n)])  30.7 us
    ppermute x2, waiting for transfers between devices, swap_both(): return lax.ppermute(x, ('layer', 'token'), [(i, i ^ 3) for i in range(4)])  13.6 us
    dot_general x8, matrix products, dot(): return jnp.dot(a, b, preferred_element_type=F32)  4.37 us
    dot_general x8, matrix products, dot_t(): lax.dot_general(a, b, (((1,), (1,)), ((), ())), preferred_element_type=F32)  3.41 us
    dot_general x2, matrix products, dot_rows(): lax.dot_general(a, b, (((0,), (0,)), ((), ())), preferred_element_type=F32)  3.31 us
  transfers between devices with their start and end apart: 36, of which 17 were waited for; matrix products, arithmetic and copies ran while one was open for 15% of the time, Pallas kernels for 0%

profile of v1, /device:TPU:0, one launch (start us, length us, event | category | flops | bytes accessed | tf_op | source)
XLA Modules:
  0.0 101.9 jit_solution(5637078681061742103)
XLA Ops:
  1.2 2.0 %dynamic-slice_bitcast_fusion = (bf16[56,1792]{1,0:T(8,128)(2,1)S(1)}, bf16[56,1792]{1,0:T(8,128)(2,1)S(1)}, bf16[56,1792]{1,0:T(8,128)(2,1)}, bf16[56,1792]{1,0:T(8,128)(2,1)S(1)}) fusion(bf16[1,224,3584]{2,1,0:T(8,128)(2,1)} %param.6, s32[]{:T(128)S(6)} %select_n.191, s32[]{:T(128)S(6)} %select_n.188, s32[]{:T(128)S(6)} %select_n.189, s32[]{:T(128)S(6)} %select_n.187, ...), kind=kLoop, calls=%fused_computation.51 | loop fusion | bytes 1605652 | tf_op jit(solution)/shard_map/dynamic_slice | solution.py:134
  3.2 2.6 %collective-permute-start = (bf16[56,1792]{1,0:T(8,128)(2,1)S(1)}, bf16[56,1792]{1,0:T(8,128)(2,1)S(1)}, u32[]{:S(2)}, u32[]{:S(2)}) collective-permute-start(bf16[56,1792]{1,0:T(8,128)(2,1)S(1)} %get-tuple-element.24), channel_id=1, source_target_pairs={{0,1},{1,0},{2,3},{3,2},{4,5},{5,4},{6,7},{7,6},{8,9},{9,8},{10,11... | collective-permute-start | bytes 602120 | tf_op jit(solution)/shard_map/ppermute | solution.py:82
  10.5 13.6 %collective-permute-done.3 = bf16[56,1792]{1,0:T(8,128)(2,1)} collective-permute-done((bf16[56,1792]{1,0:T(8,128)(2,1)}, bf16[56,1792]{1,0:T(8,128)(2,1)}, u32[]{:S(2)}, u32[]{:S(2)}) %collective-permute-start.3) | collective-permute-done | bytes 200736 | tf_op jit(solution)/shard_map/ppermute | solution.py:94
  25.5 1.8 %collective-permute-start.7 = (bf16[112,256]{1,0:T(8,128)(2,1)S(1)}, bf16[112,256]{1,0:T(8,128)(2,1)S(1)}, u32[]{:S(2)}, u32[]{:S(2)}) collective-permute-start(bf16[112,256]{1,0:T(8,128)(2,1)S(1)} %get-tuple-element.99), channel_id=1, source_target_pairs={{0,1},{1,0},{2,3},{3,2},{4,5},{5,4},{6,7},{7,6},{8,9},{9,8},{10,11... | collective-permute-start | bytes 172040 | tf_op jit(solution)/shard_map/ppermute | solution.py:82
  29.5 1.8 %collective-permute-start.6 = (bf16[56,256]{1,0:T(8,128)(2,1)S(1)}, bf16[56,256]{1,0:T(8,128)(2,1)S(1)}, u32[]{:S(2)}, u32[]{:S(2)}) collective-permute-start(bf16[56,256]{1,0:T(8,128)(2,1)S(1)} %get-tuple-element.97), channel_id=1, source_target_pairs={{0,1},{1,0},{2,3},{3,2},{4,5},{5,4},{6,7},{7,6},{8,9},{9,8},{10,11... | collective-permute-start | bytes 86024 | tf_op jit(solution)/shard_map/ppermute | solution.py:82
  33.9 1.8 %collective-permute-start.13 = (bf16[56,1792]{1,0:T(8,128)(2,1)S(1)}, bf16[56,1792]{1,0:T(8,128)(2,1)S(1)}, u32[]{:S(2)}, u32[]{:S(2)}) collective-permute-start(bf16[56,1792]{1,0:T(8,128)(2,1)S(1)} %convolution_convert_fusion.3), channel_id=1, source_target_pairs={{0,2},{2,0},{4,6},{6,4},{8,10},{10,8},{12,14},{14,12},{1,3},{3,1},... | collective-permute-start | bytes 602120 | tf_op jit(solution)/shard_map/ppermute | solution.py:82
  36.4 1.7 %collective-permute-start.10 = (f32[480]{0:T(512)S(1)}, f32[480]{0:T(512)S(1)}, u32[]{:S(2)}, u32[]{:S(2)}) collective-permute-start(f32[480]{0:T(512)S(1)} %pad_maximum_fusion.5), channel_id=1, source_target_pairs={{0,1},{1,0},{2,3},{3,2},{4,5},{5,4},{6,7},{7,6},{8,9},{9,8},{10,11... | collective-permute-start | bytes 5768 | tf_op jit(solution)/shard_map/ppermute | solution.py:82
  39.0 1.6 %collective-permute-start.23 = (bf16[56,1792]{1,0:T(8,128)(2,1)S(1)}, bf16[56,1792]{1,0:T(8,128)(2,1)S(1)}, u32[]{:S(2)}, u32[]{:S(2)}) collective-permute-start(bf16[56,1792]{1,0:T(8,128)(2,1)S(1)} %convolution_convert_fusion.1), channel_id=1, source_target_pairs={{0,4},{2,6},{4,0},{6,2},{8,12},{10,14},{12,8},{14,10},{1,5},{3,7},... | collective-permute-start | bytes 602120 | tf_op jit(solution)/shard_map/ppermute | solution.py:82
  41.8 2.0 %collective-permute-done.11 = bf16[56,1792]{1,0:T(8,128)(2,1)S(1)} collective-permute-done((bf16[56,1792]{1,0:T(8,128)(2,1)S(1)}, bf16[56,1792]{1,0:T(8,128)(2,1)S(1)}, u32[]{:S(2)}, u32[]{:S(2)}) %collective-permute-start.11) | collective-permute-done | bytes 200736 | tf_op jit(solution)/shard_map/ppermute | solution.py:82
  44.3 1.6 %collective-permute-start.12 = (bf16[56,1792]{1,0:T(8,128)(2,1)S(1)}, bf16[56,1792]{1,0:T(8,128)(2,1)S(1)}, u32[]{:S(2)}, u32[]{:S(2)}) collective-permute-start(bf16[56,1792]{1,0:T(8,128)(2,1)S(1)} %add_convert_fusion), channel_id=1, source_target_pairs={{0,4},{2,6},{4,0},{6,2},{8,12},{10,14},{12,8},{14,10},{1,5},{3,7},... | collective-permute-start | bytes 602120 | tf_op jit(solution)/shard_map/ppermute | solution.py:82
  46.9 1.9 %collective-permute-start.24 = (bf16[56,1792]{1,0:T(8,128)(2,1)S(1)}, bf16[56,1792]{1,0:T(8,128)(2,1)S(1)}, u32[]{:S(2)}, u32[]{:S(2)}) collective-permute-start(bf16[56,1792]{1,0:T(8,128)(2,1)S(1)} %fusion.4), channel_id=1, source_target_pairs={{0,2},{2,0},{4,6},{6,4},{8,10},{10,8},{12,14},{14,12},{1,3},{3,1},... | collective-permute-start | bytes 602120 | tf_op jit(solution)/shard_map/ppermute | solution.py:82
  48.8 3.2 %collective-permute-done.12 = bf16[56,1792]{1,0:T(8,128)(2,1)S(1)} collective-permute-done((bf16[56,1792]{1,0:T(8,128)(2,1)S(1)}, bf16[56,1792]{1,0:T(8,128)(2,1)S(1)}, u32[]{:S(2)}, u32[]{:S(2)}) %collective-permute-start.12) | collective-permute-done | bytes 200736 | tf_op jit(solution)/shard_map/ppermute | solution.py:82
  52.2 3.3 %collective-permute-start.14 = (bf16[56,896]{1,0:T(8,128)(2,1)S(1)}, bf16[56,896]{1,0:T(8,128)(2,1)S(1)}, u32[]{:S(2)}, u32[]{:S(2)}) collective-permute-start(bf16[56,896]{1,0:T(8,128)(2,1)S(1)} %dynamic-slice_convert_fusion.1), channel_id=1, source_target_pairs={{0,8},{2,10},{4,12},{6,14},{8,0},{10,2},{12,4},{14,6},{1,9},{3,11}... | collective-permute-start | bytes 301064 | tf_op jit(solution)/shard_map/ppermute | solution.py:82
  56.2 6.4 %collective-permute-done.14 = bf16[56,896]{1,0:T(8,128)(2,1)S(1)} collective-permute-done((bf16[56,896]{1,0:T(8,128)(2,1)S(1)}, bf16[56,896]{1,0:T(8,128)(2,1)S(1)}, u32[]{:S(2)}, u32[]{:S(2)}) %collective-permute-start.14) | collective-permute-done | bytes 100384 | tf_op jit(solution)/shard_map/ppermute | solution.py:82
  64.9 2.0 %collective-permute-start.26 = (bf16[56,896]{1,0:T(8,128)(2,1)S(1)}, bf16[56,896]{1,0:T(8,128)(2,1)S(1)}, u32[]{:S(2)}, u32[]{:S(2)}) collective-permute-start(bf16[56,896]{1,0:T(8,128)(2,1)S(1)} %multiply_convert_fusion), channel_id=1, source_target_pairs={{0,8},{2,10},{4,12},{6,14},{8,0},{10,2},{12,4},{14,6},{1,9},{3,11}... | collective-permute-start | bytes 301064 | tf_op jit(solution)/shard_map/ppermute | solution.py:82
  70.1 3.3 %collective-permute-done.26 = bf16[56,896]{1,0:T(8,128)(2,1)S(1)} collective-permute-done((bf16[56,896]{1,0:T(8,128)(2,1)S(1)}, bf16[56,896]{1,0:T(8,128)(2,1)S(1)}, u32[]{:S(2)}, u32[]{:S(2)}) %collective-permute-start.26) | collective-permute-done | bytes 100384 | tf_op jit(solution)/shard_map/ppermute | solution.py:82
  75.1 2.1 %collective-permute-start.18 = (bf16[56,1792]{1,0:T(8,128)(2,1)S(1)}, bf16[56,1792]{1,0:T(8,128)(2,1)S(1)}, u32[]{:S(2)}, u32[]{:S(2)}) collective-permute-start(bf16[56,1792]{1,0:T(8,128)(2,1)S(1)} %get-tuple-element.77), channel_id=1, source_target_pairs={{0,4},{2,6},{4,0},{6,2},{8,12},{10,14},{12,8},{14,10},{1,5},{3,7},... | collective-permute-start | bytes 602120 | tf_op jit(solution)/shard_map/ppermute | solution.py:82
  77.9 3.3 %collective-permute-done.28 = bf16[56,1792]{1,0:T(8,128)(2,1)S(1)} collective-permute-done((bf16[56,1792]{1,0:T(8,128)(2,1)S(1)}, bf16[56,1792]{1,0:T(8,128)(2,1)S(1)}, u32[]{:S(2)}, u32[]{:S(2)}) %collective-permute-start.28) | collective-permute-done | bytes 200736 | tf_op jit(solution)/shard_map/ppermute | solution.py:82
  81.4 4.5 %collective-permute-done.18 = bf16[56,1792]{1,0:T(8,128)(2,1)S(1)} collective-permute-done((bf16[56,1792]{1,0:T(8,128)(2,1)S(1)}, bf16[56,1792]{1,0:T(8,128)(2,1)S(1)}, u32[]{:S(2)}, u32[]{:S(2)}) %collective-permute-start.18) | collective-permute-done | bytes 200736 | tf_op jit(solution)/shard_map/ppermute | solution.py:82
  86.5 1.6 %collective-permute-done.29 = bf16[56,1792]{1,0:T(8,128)(2,1)S(1)} collective-permute-done((bf16[56,1792]{1,0:T(8,128)(2,1)S(1)}, bf16[56,1792]{1,0:T(8,128)(2,1)S(1)}, u32[]{:S(2)}, u32[]{:S(2)}) %collective-permute-start.29) | collective-permute-done | bytes 200736 | tf_op jit(solution)/shard_map/ppermute | solution.py:82
  88.5 3.1 %collective-permute-done.20 = bf16[56,1792]{1,0:T(8,128)(2,1)S(1)} collective-permute-done((bf16[56,1792]{1,0:T(8,128)(2,1)S(1)}, bf16[56,1792]{1,0:T(8,128)(2,1)S(1)}, u32[]{:S(2)}, u32[]{:S(2)}) %collective-permute-start.20) | collective-permute-done | bytes 200736 | tf_op jit(solution)/shard_map/ppermute | solution.py:82
  93.1 3.8 %collective-permute-done.30 = bf16[224,256]{1,0:T(8,128)(2,1)S(1)} collective-permute-done((bf16[224,256]{1,0:T(8,128)(2,1)S(1)}, bf16[224,256]{1,0:T(8,128)(2,1)S(1)}, u32[]{:S(2)}, u32[]{:S(2)}) %collective-permute-start.30) | collective-permute-done | bytes 114720 | tf_op jit(solution)/shard_map/ppermute | solution.py:82
  98.5 1.6 %fusion.2 = bf16[1,1792,256]{2,1,0:T(8,128)(2,1)} fusion(bf16[448,1792]{1,0:T(8,128)(2,1)S(1)} %constant_dynamic-update-slice_fusion, bf16[448,256]{1,0:T(8,128)(2,1)S(1)} %constant_dynamic-update-slice_fusion.6), kind=kOutput, calls=%fused_computation.4 | convolution fusion | flops 411500544 | bytes 2752512 | tf_op jit(solution)/shard_map/dot_general | solution.py:106
  100.2 1.7 %fusion.1 = bf16[1,1792,256]{2,1,0:T(8,128)(2,1)} fusion(bf16[448,1792]{1,0:T(8,128)(2,1)S(1)} %constant_dynamic-update-slice_fusion.11, bf16[448,256]{1,0:T(8,128)(2,1)S(1)} %constant_dynamic-update-slice_fusion.20, f32[256]{0:T(256)S(1)} %get-tuple-element.44, bf16[1,1792,256]{2,1,0:T(8,128)(2,1)S(1)} %copy-done), kind=kOutput, calls=%fused_computation.3 | convolution fusion | flops 412876800 | bytes 3671040 | tf_op jit(solution)/shard_map/dot_general | solution.py:106
  (127 shorter events, 28.3 us)
Async XLA Ops:
  3.2 25.9 %collective-permute-start = (bf16[56,1792]{1,0:T(8,128)(2,1)S(1)}, bf16[56,1792]{1,0:T(8,128)(2,1)S(1)}, u32[]{:S(2)}, u32[]{:S(2)}) collective-permute-start(bf16[56,1792]{1,0:T(8,128)(2,1)S(1)} %get-tuple-element.24), channel_id=1, source_target_pairs={{0,1},{1,0},{2,3},{3,2},{4,5},{5,4},{6,7},{7,6},{8,9},{9,8},{10,11... | collective-permute-start | bytes 602120 | tf_op jit(solution)/shard_map/ppermute | solution.py:82
  5.9 19.6 %collective-permute-start.1 = (bf16[56,1792]{1,0:T(8,128)(2,1)S(1)}, bf16[56,1792]{1,0:T(8,128)(2,1)S(1)}, u32[]{:S(2)}, u32[]{:S(2)}) collective-permute-start(bf16[56,1792]{1,0:T(8,128)(2,1)S(1)} %get-tuple-element.25), channel_id=1, source_target_pairs={{0,1},{1,0},{2,3},{3,2},{4,5},{5,4},{6,7},{7,6},{8,9},{9,8},{10,11... | collective-permute-start | bytes 602120 | tf_op jit(solution)/shard_map/ppermute | solution.py:82
  5.9 21.7 %collective-permute-start.2 = (bf16[56,1792]{1,0:T(8,128)(2,1)S(1)}, bf16[56,1792]{1,0:T(8,128)(2,1)}, u32[]{:S(2)}, u32[]{:S(2)}) collective-permute-start(bf16[56,1792]{1,0:T(8,128)(2,1)S(1)} %get-tuple-element.26), channel_id=1, source_target_pairs={{0,17},{1,16},{16,1},{17,0},{2,19},{3,18},{18,3},{19,2},{4,21},{5,... | collective-permute-start | bytes 602120 | tf_op jit(solution)/shard_map/ppermute | solution.py:94
  7.3 16.8 %collective-permute-start.3 = (bf16[56,1792]{1,0:T(8,128)(2,1)}, bf16[56,1792]{1,0:T(8,128)(2,1)}, u32[]{:S(2)}, u32[]{:S(2)}) collective-permute-start(bf16[56,1792]{1,0:T(8,128)(2,1)} %get-tuple-element.27), channel_id=1, source_target_pairs={{0,17},{1,16},{16,1},{17,0},{2,19},{3,18},{18,3},{19,2},{4,21},{5,... | collective-permute-start | bytes 602120 | tf_op jit(solution)/shard_map/ppermute | solution.py:94
  9.5 26.5 %collective-permute-start.9 = (f32[1,3584]{1,0:T(1,128)S(1)}, f32[1,3584]{1,0:T(1,128)S(1)}, u32[]{:S(2)}, u32[]{:S(2)}) collective-permute-start(f32[1,3584]{1,0:T(1,128)S(1)} %copy-done.5), channel_id=1, source_target_pairs={{0,16},{16,0},{1,17},{17,1},{2,18},{18,2},{3,19},{19,3},{4,20},{20... | collective-permute-start | bytes 43016 | tf_op jit(solution)/shard_map/ppermute | solution.py:82
  24.1 14.4 %collective-permute-start.21 = (bf16[1792,256]{1,0:T(8,128)(2,1)S(1)}, bf16[1792,256]{1,0:T(8,128)(2,1)S(1)}, u32[]{:S(2)}, u32[]{:S(2)}) collective-permute-start(bf16[1792,256]{1,0:T(8,128)(2,1)S(1)} %bitcast.54), channel_id=1, source_target_pairs={{0,16},{16,0},{1,17},{17,1},{2,18},{18,2},{3,19},{19,3},{4,20},{20... | collective-permute-start | bytes 2752520 | tf_op jit(solution)/shard_map/ppermute | solution.py:82
  33.9 14.9 %collective-permute-start.13 = (bf16[56,1792]{1,0:T(8,128)(2,1)S(1)}, bf16[56,1792]{1,0:T(8,128)(2,1)S(1)}, u32[]{:S(2)}, u32[]{:S(2)}) collective-permute-start(bf16[56,1792]{1,0:T(8,128)(2,1)S(1)} %convolution_convert_fusion.3), channel_id=1, source_target_pairs={{0,2},{2,0},{4,6},{6,4},{8,10},{10,8},{12,14},{14,12},{1,3},{3,1},... | collective-permute-start | bytes 602120 | tf_op jit(solution)/shard_map/ppermute | solution.py:82
  35.7 8.1 %collective-permute-start.11 = (bf16[56,1792]{1,0:T(8,128)(2,1)S(1)}, bf16[56,1792]{1,0:T(8,128)(2,1)S(1)}, u32[]{:S(2)}, u32[]{:S(2)}) collective-permute-start(bf16[56,1792]{1,0:T(8,128)(2,1)S(1)} %convolution_convert_fusion.4), channel_id=1, source_target_pairs={{0,2},{2,0},{4,6},{6,4},{8,10},{10,8},{12,14},{14,12},{1,3},{3,1},... | collective-permute-start | bytes 602120 | tf_op jit(solution)/shard_map/ppermute | solution.py:82
  39.0 7.5 %collective-permute-start.23 = (bf16[56,1792]{1,0:T(8,128)(2,1)S(1)}, bf16[56,1792]{1,0:T(8,128)(2,1)S(1)}, u32[]{:S(2)}, u32[]{:S(2)}) collective-permute-start(bf16[56,1792]{1,0:T(8,128)(2,1)S(1)} %convolution_convert_fusion.1), channel_id=1, source_target_pairs={{0,4},{2,6},{4,0},{6,2},{8,12},{10,14},{12,8},{14,10},{1,5},{3,7},... | collective-permute-start | bytes 602120 | tf_op jit(solution)/shard_map/ppermute | solution.py:82
  41.0 14.4 %collective-permute-start.22 = (bf16[56,1792]{1,0:T(8,128)(2,1)S(1)}, bf16[56,1792]{1,0:T(8,128)(2,1)S(1)}, u32[]{:S(2)}, u32[]{:S(2)}) collective-permute-start(bf16[56,1792]{1,0:T(8,128)(2,1)S(1)} %convolution_convert_fusion.2), channel_id=1, source_target_pairs={{0,4},{2,6},{4,0},{6,2},{8,12},{10,14},{12,8},{14,10},{1,5},{3,7},... | collective-permute-start | bytes 602120 | tf_op jit(solution)/shard_map/ppermute | solution.py:82
  44.3 7.8 %collective-permute-start.12 = (bf16[56,1792]{1,0:T(8,128)(2,1)S(1)}, bf16[56,1792]{1,0:T(8,128)(2,1)S(1)}, u32[]{:S(2)}, u32[]{:S(2)}) collective-permute-start(bf16[56,1792]{1,0:T(8,128)(2,1)S(1)} %add_convert_fusion), channel_id=1, source_target_pairs={{0,4},{2,6},{4,0},{6,2},{8,12},{10,14},{12,8},{14,10},{1,5},{3,7},... | collective-permute-start | bytes 602120 | tf_op jit(solution)/shard_map/ppermute | solution.py:82
  46.9 8.5 %collective-permute-start.24 = (bf16[56,1792]{1,0:T(8,128)(2,1)S(1)}, bf16[56,1792]{1,0:T(8,128)(2,1)S(1)}, u32[]{:S(2)}, u32[]{:S(2)}) collective-permute-start(bf16[56,1792]{1,0:T(8,128)(2,1)S(1)} %fusion.4), channel_id=1, source_target_pairs={{0,2},{2,0},{4,6},{6,4},{8,10},{10,8},{12,14},{14,12},{1,3},{3,1},... | collective-permute-start | bytes 602120 | tf_op jit(solution)/shard_map/ppermute | solution.py:82
  52.2 10.4 %collective-permute-start.14 = (bf16[56,896]{1,0:T(8,128)(2,1)S(1)}, bf16[56,896]{1,0:T(8,128)(2,1)S(1)}, u32[]{:S(2)}, u32[]{:S(2)}) collective-permute-start(bf16[56,896]{1,0:T(8,128)(2,1)S(1)} %dynamic-slice_convert_fusion.1), channel_id=1, source_target_pairs={{0,8},{2,10},{4,12},{6,14},{8,0},{10,2},{12,4},{14,6},{1,9},{3,11}... | collective-permute-start | bytes 301064 | tf_op jit(solution)/shard_map/ppermute | solution.py:82
  55.9 8.0 %collective-permute-start.25 = (bf16[56,896]{1,0:T(8,128)(2,1)S(1)}, bf16[56,896]{1,0:T(8,128)(2,1)S(1)}, u32[]{:S(2)}, u32[]{:S(2)}) collective-permute-start(bf16[56,896]{1,0:T(8,128)(2,1)S(1)} %dynamic-slice_convert_fusion), channel_id=1, source_target_pairs={{0,8},{2,10},{4,12},{6,14},{8,0},{10,2},{12,4},{14,6},{1,9},{3,11}... | collective-permute-start | bytes 301064 | tf_op jit(solution)/shard_map/ppermute | solution.py:82
  62.7 12.3 %collective-permute-start.17 = (bf16[56,896]{1,0:T(8,128)(2,1)S(1)}, bf16[56,896]{1,0:T(8,128)(2,1)S(1)}, u32[]{:S(2)}, u32[]{:S(2)}) collective-permute-start(bf16[56,896]{1,0:T(8,128)(2,1)S(1)} %multiply_convert_fusion.1), channel_id=1, source_target_pairs={{0,8},{2,10},{4,12},{6,14},{8,0},{10,2},{12,4},{14,6},{1,9},{3,11}... | collective-permute-start | bytes 301064 | tf_op jit(solution)/shard_map/ppermute | solution.py:82
  62.8 14.4 %collective-permute-start.15 = (bf16[56,1792]{1,0:T(8,128)(2,1)}, bf16[56,1792]{1,0:T(8,128)(2,1)S(1)}, u32[]{:S(2)}, u32[]{:S(2)}) collective-permute-start(bf16[56,1792]{1,0:T(8,128)(2,1)} %collective-permute-done.2), channel_id=1, source_target_pairs={{0,16},{16,0},{1,17},{17,1},{2,18},{18,2},{3,19},{19,3},{4,20},{20... | collective-permute-start | bytes 602120 | tf_op jit(solution)/shard_map/ppermute | solution.py:82
  64.9 8.5 %collective-permute-start.26 = (bf16[56,896]{1,0:T(8,128)(2,1)S(1)}, bf16[56,896]{1,0:T(8,128)(2,1)S(1)}, u32[]{:S(2)}, u32[]{:S(2)}) collective-permute-start(bf16[56,896]{1,0:T(8,128)(2,1)S(1)} %multiply_convert_fusion), channel_id=1, source_target_pairs={{0,8},{2,10},{4,12},{6,14},{8,0},{10,2},{12,4},{14,6},{1,9},{3,11}... | collective-permute-start | bytes 301064 | tf_op jit(solution)/shard_map/ppermute | solution.py:82
  66.9 8.2 %collective-permute-start.34 = (bf16[224,256]{1,0:T(8,128)(2,1)S(1)}, bf16[224,256]{1,0:T(8,128)(2,1)S(1)}, u32[]{:S(2)}, u32[]{:S(2)}) collective-permute-start(bf16[224,256]{1,0:T(8,128)(2,1)S(1)} %get-tuple-element.85), channel_id=1, source_target_pairs={{0,16},{16,0},{1,17},{17,1},{2,18},{18,2},{3,19},{19,3},{4,20},{20... | collective-permute-start | bytes 344072 | tf_op jit(solution)/shard_map/ppermute | solution.py:82
  69.8 8.1 %collective-permute-start.16 = (bf16[56,1792]{1,0:T(8,128)(2,1)}, bf16[56,1792]{1,0:T(8,128)(2,1)S(1)}, u32[]{:S(2)}, u32[]{:S(2)}) collective-permute-start(bf16[56,1792]{1,0:T(8,128)(2,1)} %collective-permute-done.3), channel_id=1, source_target_pairs={{0,16},{16,0},{1,17},{17,1},{2,18},{18,2},{3,19},{19,3},{4,20},{20... | collective-permute-start | bytes 602120 | tf_op jit(solution)/shard_map/ppermute | solution.py:82
  73.5 7.7 %collective-permute-start.28 = (bf16[56,1792]{1,0:T(8,128)(2,1)S(1)}, bf16[56,1792]{1,0:T(8,128)(2,1)S(1)}, u32[]{:S(2)}, u32[]{:S(2)}) collective-permute-start(bf16[56,1792]{1,0:T(8,128)(2,1)S(1)} %pad_maximum_fusion.3), channel_id=1, source_target_pairs={{0,2},{2,0},{4,6},{6,4},{8,10},{10,8},{12,14},{14,12},{1,3},{3,1},... | collective-permute-start | bytes 602120 | tf_op jit(solution)/shard_map/ppermute | solution.py:82
  75.0 11.4 %collective-permute-start.27 = (bf16[56,1792]{1,0:T(8,128)(2,1)S(1)}, bf16[56,1792]{1,0:T(8,128)(2,1)S(1)}, u32[]{:S(2)}, u32[]{:S(2)}) collective-permute-start(bf16[56,1792]{1,0:T(8,128)(2,1)S(1)} %pad_maximum_fusion.3), channel_id=1, source_target_pairs={{0,4},{2,6},{4,0},{6,2},{8,12},{10,14},{12,8},{14,10},{1,5},{3,7},... | collective-permute-start | bytes 602120 | tf_op jit(solution)/shard_map/ppermute | solution.py:82
  75.1 10.8 %collective-permute-start.18 = (bf16[56,1792]{1,0:T(8,128)(2,1)S(1)}, bf16[56,1792]{1,0:T(8,128)(2,1)S(1)}, u32[]{:S(2)}, u32[]{:S(2)}) collective-permute-start(bf16[56,1792]{1,0:T(8,128)(2,1)S(1)} %get-tuple-element.77), channel_id=1, source_target_pairs={{0,4},{2,6},{4,0},{6,2},{8,12},{10,14},{12,8},{14,10},{1,5},{3,7},... | collective-permute-start | bytes 602120 | tf_op jit(solution)/shard_map/ppermute | solution.py:82
  77.2 11.3 %collective-permute-start.19 = (bf16[56,1792]{1,0:T(8,128)(2,1)S(1)}, bf16[56,1792]{1,0:T(8,128)(2,1)S(1)}, u32[]{:S(2)}, u32[]{:S(2)}) collective-permute-start(bf16[56,1792]{1,0:T(8,128)(2,1)S(1)} %get-tuple-element.77), channel_id=1, source_target_pairs={{0,2},{2,0},{4,6},{6,4},{8,10},{10,8},{12,14},{14,12},{1,3},{3,1},... | collective-permute-start | bytes 602120 | tf_op jit(solution)/shard_map/ppermute | solution.py:82
  93.0 7.1 %collective-permute-start.33 = (bf16[224,1792]{1,0:T(8,128)(2,1)S(1)}, bf16[224,1792]{1,0:T(8,128)(2,1)S(1)}, u32[]{:S(2)}, u32[]{:S(2)}) collective-permute-start(bf16[224,1792]{1,0:T(8,128)(2,1)S(1)} %pad_maximum_fusion.1), channel_id=1, source_target_pairs={{0,16},{16,0},{1,17},{17,1},{2,18},{18,2},{3,19},{19,3},{4,20},{20... | collective-permute-start | bytes 2408456 | tf_op jit(solution)/shard_map/ppermute | solution.py:82
  (18 other events, 90.5 us)
